TPU v7x, 512 devices: a whole 4x8x8 slice. The times are simulated.
512 devices in a mesh: expert: 32 (over x, z_hi, core), tensor: 8 (over y), dp: 2 (over z_lo).
Axes of the slice: x: 4, y: 8, z: 8 (z_hi: 4, z_lo: 2; z = z_hi * 2 + z_lo), core: 2. Of those that a mesh axis runs over, the one named last changes fastest.
Arguments:
- tokens: bfloat16 [6144, 5120], P(('dp', 'expert'), 'tensor'), parts along dimension 0, may hold values from -6 to 6
- routes: int32 [6144, 6], P(('dp', 'expert')), parts along dimension 0, may hold values from 0 to 31, all different within a row; in each aligned block of 96 rows (0 to 95, 96 to 191, ...) at most 18 rows name the same one
- gates: float32 [6144, 6], P(('dp', 'expert')), parts along dimension 0, may hold values from 0.05 to 0.6
- gate_up: bfloat16 [32, 5120, 2, 1024], P('expert', None, None, 'tensor'), may hold values from -0.078125 to 0.078125
- down_weight: bfloat16 [32, 5120, 1024], P('expert', None, 'tensor'), may hold values from -0.1875 to 0.1875
- old_map: int32 [32], replicated, may hold values from 0 to 31, each once
- new_map: int32 [32], replicated, may hold values from 0 to 31, each once
Outputs:
- mixed: bfloat16 [6144, 5120], P(('dp', 'expert'), 'tensor'), parts along dimension 0
There are 2 independent parts, one for each index of `dp`. A program takes and returns all parts, laid end to end along the dimension named above; an argument that names none is the same for every part. Nothing has to cross between parts.
Inputs may be any that keep to these rules, and one draw needn't show every extreme that they name: `routes`: each row names 6 different slots; in each aligned block of 96 rows (the rows of one index of expert) no slot is named by more than 18 rows; since each row names 6 different slots, every slot is then named by exactly 18 rows of every block. `old_map`: each expert appears exactly once. `new_map`: each expert appears exactly once.
All inputs are finite; a program needn't handle non-finite values.
Results may differ from a plain program's by a relative error of at most 0.0058.
Values may be sent and summed in bfloat16 or wider, within the bound.
No kernel may reach another device: no remote copies, remote signals or barrier semaphores. Data moves between devices by JAX's collectives and lax.ppermute only.
A program may use at most 64 MiB of HBM per device.

v0:
```python
import jax
import jax.numpy as jnp
from jax import lax
from jax.sharding import Mesh
from jax.sharding import PartitionSpec as P

EXPERT = ("expert_0", "expert_1", "expert_2")
DP_EXPERT = ("dp", "expert_0", "expert_1", "expert_2")


def in_blocks(x, dim, size):
    lengths = x.shape
    parts = x.reshape(*lengths[:dim], size, lengths[dim] // size, *lengths[dim + 1 :])
    return jnp.moveaxis(parts, dim, 0)


def laid_out(parts, dim):
    parts = jnp.moveaxis(parts, 0, dim)
    lengths = parts.shape
    return parts.reshape(*lengths[:dim], lengths[dim] * lengths[dim + 1], *lengths[dim + 2 :])


def exchange_in_order(parts, axes, order):
    lengths = [lax.axis_size(a) for a in axes]
    parts = parts.reshape(*lengths, *parts.shape[1:])
    for k in order:
        parts = lax.all_to_all(parts, axes[k], split_axis=k, concat_axis=k, tiled=True)
    return parts.reshape(-1, *parts.shape[len(axes) :])


def core_and_chips(x, groups, order, split_dim, concat_dim):
    size = lax.axis_size(groups[0]) * lax.axis_size(groups[1])
    parts = in_blocks(x, split_dim, size)
    return laid_out(exchange_in_order(parts, groups, order), concat_dim)


def from_everyone(x, axis):
    size = lax.axis_size(axis)
    return lax.all_to_all(jnp.broadcast_to(x[None], (size, *x.shape)), axis, 0, 0, tiled=True)


def collect(x, axis, dim):
    parts = from_everyone(x, axis)
    return laid_out(parts, dim)


def local(tokens, routes, gates, gate_up, down_weight, old_map, new_map):
    experts = lax.axis_size(EXPERT)
    tensor_count = lax.axis_size("tensor")
    tok_rows = tokens.shape[0]
    feature_part = tokens.shape[1]
    picks_row = routes.shape[1]
    capacity = (tok_rows * picks_row + experts - 1) // experts
    width = gate_up.shape[1]
    hidden = down_weight.shape[2]
    buffer_rows = experts * capacity
    slot_ids = jnp.arange(experts, dtype=jnp.int32)
    holder = jnp.sum(jnp.where(new_map[:, None] == old_map[None, :], slot_ids[None, :], 0), axis=1)
    weight_in = gate_up.reshape(width, 2 * hidden)
    weight_out = down_weight.reshape(width, hidden)
    target = jnp.sum(
        jnp.where(routes[:, :, None] == slot_ids[None, None, :], holder[None, None, :], 0), axis=2
    )
    flat_target = target.reshape(-1)
    onehot = (flat_target[:, None] == slot_ids[None, :]).astype(jnp.int32)
    earlier = jnp.cumsum(onehot, axis=0) - onehot
    position = jnp.sum(earlier * onehot, axis=1)
    slot_index = flat_target * capacity + position
    columns = jnp.arange(buffer_rows, dtype=jnp.int32)
    matches = (slot_index[:, None] == columns[None, :]).reshape(tok_rows, picks_row, buffer_rows)
    assign = jnp.sum(matches.astype(jnp.float32), axis=1).astype(jnp.bfloat16)
    combine_weights = jnp.sum(jnp.where(matches, gates[:, :, None], 0.0), axis=1)
    outgoing = lax.dot_general(
        assign, tokens, (((0,), (0,)), ((), ())), preferred_element_type=jnp.float32
    )
    outgoing = outgoing.astype(jnp.bfloat16).reshape(experts, capacity, feature_part)
    arrived = core_and_chips(outgoing, (("expert_0", "expert_1"), "expert_2"), (1, 0), 0, 0)
    piece = lax.all_gather(arrived, "tensor", axis=2, tiled=True)
    flat_piece = piece.reshape(buffer_rows, piece.shape[2])
    projected = jnp.dot(flat_piece, weight_in, preferred_element_type=jnp.float32)
    activation = (jax.nn.silu(projected[:, :hidden]) * projected[:, hidden:]).astype(jnp.bfloat16)
    down_parts = weight_out.reshape(tensor_count, width // tensor_count, hidden)
    down_mine = lax.all_to_all(
        down_parts, "tensor", split_axis=0, concat_axis=2, tiled=True
    ).reshape(width // tensor_count, tensor_count * hidden)
    summed = lax.dot_general(
        collect(activation, "tensor", 1),
        down_mine,
        (((1,), (1,)), ((), ())),
        preferred_element_type=jnp.float32,
    )
    expert_out = summed.astype(jnp.bfloat16).reshape(experts, capacity, feature_part)
    returned = lax.all_to_all(expert_out, EXPERT, split_axis=0, concat_axis=0, tiled=True)
    gathered_back = returned.reshape(buffer_rows, feature_part).astype(jnp.float32)
    mixed = jnp.dot(
        combine_weights,
        gathered_back,
        precision=lax.Precision.HIGHEST,
        preferred_element_type=jnp.float32,
    )
    return mixed.astype(jnp.bfloat16)


def solution(mesh):
    split = Mesh(
        mesh.devices.reshape(4, 4, 2, mesh.shape["tensor"], mesh.shape["dp"]),
        ("expert_0", "expert_1", "expert_2", "tensor", "dp"),
    )
    in_specs = (
        P(DP_EXPERT, "tensor"),
        P(DP_EXPERT, None),
        P(DP_EXPERT, None),
        P(EXPERT, None, None, "tensor"),
        P(EXPERT, None, "tensor"),
        P(),
        P(),
    )
    out_specs = P(DP_EXPERT, "tensor")
    return jax.shard_map(local, mesh=split, in_specs=in_specs, out_specs=out_specs, check_vma=False)
```

profile of v0, /device:TPU:64, one launch (start us, length us, event | category | flops | bytes accessed | tf_op | source)
XLA Modules:
  0.0 253.1 jit_solution(2696037991912060983)
XLA Ops:
  6.5 0.0 copy-start
  6.5 0.0 all-gather.2.cloned.1.call-start
  6.5 0.9 select_reduce_fusion.2
  7.4 0.8 select_reduce_fusion.1
  8.2 0.1 copy.37
  8.3 0.1 eq.68
  8.5 1.5 reduce-window.6
  10.0 0.3 slice_reduce_fusion
  10.2 0.1 bitcast_bitcast_fusion
  10.4 0.1 reduce_sum.50
  10.5 0.1 copy.40
  10.6 1.1 convert_reduce_fusion
  11.7 0.0 copy-done
  11.7 0.4 convolution_convert_fusion.1
  12.1 0.2 reshape_reshape_reshape.3
  12.3 0.1 copy.41
  12.4 4.3 %all_to_all.35 = bf16[16,2,1,18,640]{4,0,3,2,1:T(8,128)(2,1)S(1)} all-to-all(bf16[16,2,1,18,640]{4,0,3,2,1:T(8,128)(2,1)S(1)} %copy.41), channel_id=1, replica_groups=mesh['expert_0'=4,'expert_1'=4,'expert_2'=2,'tensor'=8,'dp'=2] {'expert_2'}, dimensions={1} | all-to-all | bytes 1474560 | tf_op jit(solution)/shard_map/all_to_all | solution.py:27
  16.7 0.6 copy.42
  17.3 35.1 %all_to_all.36 = bf16[16,2,1,18,640]{4,1,3,2,0:T(2,128)(2,1)S(1)} all-to-all(bf16[16,2,1,18,640]{4,1,3,2,0:T(2,128)(2,1)S(1)} %copy.42), channel_id=1, replica_groups=mesh['expert_0'=4,'expert_1'=4,'expert_2'=2,'tensor'=8,'dp'=2] {'expert_..., dimensions={0} | all-to-all | bytes 1474560 | tf_op jit(solution)/shard_map/all_to_all | solution.py:27
  52.4 0.5 copy.43
  52.9 1.1 reshape_reshape.6
  54.0 0.0 all-gather.2.cloned.1.call-update
  54.1 7.1 %all-to-all-start.3 = ((bf16[8,640,128]{2,1,0:T(8,128)(2,1)}), bf16[8,640,128]{2,1,0:T(8,128)(2,1)S(1)}, u32[]{:S(2)}, u32[]{:S(2)}) async-start(bf16[8,640,128]{2,1,0:T(8,128)(2,1)} %bitcast.2), calls=%async_computation.3 | async-start | bytes 2621440 | tf_op jit(solution)/shard_map/all_to_all | solution.py:83
  61.2 86.8 %all-gather.2.cloned.1.call-done = bf16[32,18,5120]{2,0,1:T(8,128)(2,1)} async-done(((bf16[32,18,640]{2,0,1:T(8,128)(2,1)}), bf16[32,18,5120]{2,0,1:T(8,128)(2,1)}) %all-gather.2.cloned.1.call-update) | async-done | bytes 5898256 | tf_op jit(solution)/shard_map/all_gather | solution.py:78
  148.0 9.2 %copy.44 = bf16[32,18,5120]{2,1,0:T(8,128)(2,1)} copy(bf16[32,18,5120]{2,0,1:T(8,128)(2,1)} %all-gather.2.cloned.1.call-done) | data formatting | bytes 11796480 | tf_op jit(solution)/shard_map/all_gather | solution.py:78
  157.1 8.8 %reshape.57 = bf16[576,5120]{1,0:T(8,128)(2,1)} reshape(bf16[32,18,5120]{2,1,0:T(8,128)(2,1)} %copy.44) | data formatting | bytes 11796480 | tf_op jit(solution)/shard_map/reshape | solution.py:79
  165.9 5.2 %fusion = f32[576,256]{1,0:T(8,128)S(1)} fusion(bf16[576,5120]{1,0:T(8,128)(2,1)} %reshape.57, bf16[640,8,2,128]{3,2,1,0:T(2,128)(2,1)} %bitcast.42), kind=kOutput, calls=%fused_computation | convolution fusion | flops 1509949440 | bytes 9109504 | tf_op jit(solution)/shard_map/dot_general | solution.py:80
  171.1 0.1 fusion.5
  171.2 0.0 all-to-all-done.3
  171.2 1.2 broadcast_in_dim.58
  172.4 4.5 %all-to-all-start.2 = ((bf16[8,576,128]{2,1,0:T(8,128)(2,1)}), bf16[8,576,128]{2,1,0:T(8,128)(2,1)}, u32[]{:S(2)}, u32[]{:S(2)}) async-start(bf16[8,576,128]{2,1,0:T(8,128)(2,1)} %broadcast_in_dim.58), calls=%async_computation.2 | async-start | bytes 2359296 | tf_op jit(solution)/shard_map/all_to_all | solution.py:39
  176.9 0.7 copy.46
  177.6 31.1 %all-to-all-done.2 = bf16[8,576,128]{2,1,0:T(8,128)(2,1)} async-done(((bf16[8,576,128]{2,1,0:T(8,128)(2,1)}), bf16[8,576,128]{2,1,0:T(8,128)(2,1)}, u32[]{:S(2)}, u32[]{:S(2)}) %all-to-all-start.2) | async-done | bytes 1179680 | tf_op jit(solution)/shard_map/all_to_all | solution.py:39
  208.8 3.3 %convolution_convert_fusion = bf16[576,640]{1,0:T(8,128)(2,1)} fusion(bf16[640,1024]{0,1:T(8,128)(2,1)S(1)} %bitcast.40, bf16[8,576,128]{2,1,0:T(8,128)(2,1)} %all-to-all-done.2), kind=kOutput, calls=%fused_computation.6 | convolution fusion | flops 755343360 | bytes 3227648 | tf_op jit(solution)/shard_map/dot_general | solution.py:86
  212.0 1.3 reshape.61
  213.3 31.5 %all_to_all.37 = bf16[32,18,640]{2,1,0:T(8,128)(2,1)S(1)} all-to-all(bf16[32,18,640]{2,1,0:T(8,128)(2,1)S(1)} %reshape.61), channel_id=1, replica_groups=mesh['expert_0'=4,'expert_1'=4,'expert_2'=2,'tensor'=8,'dp'=2] {'expert_..., dimensions={0} | all-to-all | bytes 1474560 | tf_op jit(solution)/shard_map/all_to_all | solution.py:93
  244.8 0.2 reshape.62
  245.0 1.2 convolution_convert_fusion.2
  (5 shorter events, 0.1 us)
Async XLA Ops:
  6.5 5.1 %copy-start = (bf16[96,640]{1,0:T(8,128)(2,1)S(1)}, bf16[96,640]{1,0:T(8,128)(2,1)}, u32[]{:S(2)}) copy-start(bf16[96,640]{1,0:T(8,128)(2,1)} %param.7) | copy-start | bytes 368644
  6.5 141.4 %all-gather.2.cloned.1.call-start = ((), (), s32[]{:S(2)}) async-start(), calls=%async_computation.5 | async-start | bytes 6635520 | tf_op jit(solution)/shard_map/all_gather | solution.py:78
  54.1 117.1 %all-to-all-start.3 = ((bf16[8,640,128]{2,1,0:T(8,128)(2,1)}), bf16[8,640,128]{2,1,0:T(8,128)(2,1)S(1)}, u32[]{:S(2)}, u32[]{:S(2)}) async-start(bf16[8,640,128]{2,1,0:T(8,128)(2,1)} %bitcast.2), calls=%async_computation.3 | async-start | bytes 2621440 | tf_op jit(solution)/shard_map/all_to_all | solution.py:83
  172.4 36.4 %all-to-all-start.2 = ((bf16[8,576,128]{2,1,0:T(8,128)(2,1)}), bf16[8,576,128]{2,1,0:T(8,128)(2,1)}, u32[]{:S(2)}, u32[]{:S(2)}) async-start(bf16[8,576,128]{2,1,0:T(8,128)(2,1)} %broadcast_in_dim.58), calls=%async_computation.2 | async-start | bytes 2359296 | tf_op jit(solution)/shard_map/all_to_all | solution.py:39
Sparse Core Ops, SparseCore 0:
  54.2 93.7 all-gather.1
where the time goes:
time: 254 us; the launch traced here: 253 us
  waiting for transfers between devices  118 us (46%)
  blocking collectives  70.8 us (28%)
  local copies, waits for them, and re-layouts  24.6 us (10%)
  between operations  13.5 us (5%)
  starting transfers between devices  11.7 us (5%)
  matrix products  10 us (4%)
  other arithmetic  4.47 us (2%)
    all_gather x1, waiting for transfers between devices, local(): piece = lax.all_gather(arrived, 'tensor', axis=2, tiled=True)  86.8 us
    all_to_all x2, blocking collectives, exchange_in_order(): lax.all_to_all(parts, axes[k], split_axis=k, concat_axis=k, tiled=True)  39.4 us
    all_to_all x1, blocking collectives, local(): lax.all_to_all(expert_out, EXPERT, split_axis=0, concat_axis=0, tiled=True)  31.5 us
    all_to_all x1, waiting for transfers between devices, from_everyone(): lax.all_to_all(jnp.broadcast_to(x[None], (size, *x.shape)), axis, 0, 0, t...  31.1 us
    all_gather x1, local copies, waits for them, and re-layouts, local(): piece = lax.all_gather(arrived, 'tensor', axis=2, tiled=True)  9.16 us
    reshape x1, local copies, waits for them, and re-layouts, local(): flat_piece = piece.reshape(buffer_rows, piece.shape[2])  8.78 us
    all_to_all x1, starting transfers between devices, local(): lax.all_to_all(down_parts, 'tensor', split_axis=0, concat_axis=2, tiled=T...  7.11 us
    dot_general x1, matrix products, local(): jnp.dot(flat_piece, weight_in, preferred_element_type=jnp.float32)  5.15 us
  transfers between devices with their start and end apart: 3, of which 2 were waited for; matrix products, arithmetic and copies ran while one was open for 9% of the time, Pallas kernels for 0%

commit v1 on v0

--- a/solution.py
+++ b/solution.py
@@ -75,7 +75,9 @@
     )
     outgoing = outgoing.astype(jnp.bfloat16).reshape(experts, capacity, feature_part)
     arrived = core_and_chips(outgoing, (("expert_0", "expert_1"), "expert_2"), (1, 0), 0, 0)
-    piece = lax.all_gather(arrived, "tensor", axis=2, tiled=True)
+    piece = jnp.concatenate(
+        lax.all_to_all(jnp.stack([arrived] * lax.axis_size("tensor")), "tensor", 0, 0), axis=2
+    )
     flat_piece = piece.reshape(buffer_rows, piece.shape[2])
     projected = jnp.dot(flat_piece, weight_in, preferred_element_type=jnp.float32)
     activation = (jax.nn.silu(projected[:, :hidden]) * projected[:, hidden:]).astype(jnp.bfloat16)

time: 254 us -> 298 us (1.17)
  blocking collectives: 70.8 us -> 211 us
  waiting for transfers between devices: 118 us -> 53.6 us
  between operations: 13.5 us -> 0.19 us
  local copies, waits for them, and re-layouts: 24.6 us -> 14.2 us
  starting transfers between devices: 11.7 us -> 8 us
  matrix products: 10 us -> 6.54 us
    all_to_all x0 -> x1, blocking collectives: none -> 139 us  [local(): lax.all_to_all(jnp.stack([arrived] * lax.axis_size('tensor')), 'tensor',...]
    all_gather x1 -> x0, waiting for transfers between devices: 86.8 us -> none  [local(): piece = lax.all_gather(arrived, 'tensor', axis=2, tiled=True)]
    all_to_all x1, waiting for transfers between devices: 0.01 us -> 22.6 us  [local(): lax.all_to_all(down_parts, 'tensor', split_axis=0, concat_axis=2, tiled=T...]
    all_gather x1 -> x0, local copies, waits for them, and re-layouts: 9.16 us -> none  [local(): piece = lax.all_gather(arrived, 'tensor', axis=2, tiled=True)]
    all_to_all x1, starting transfers between devices: 7.11 us -> 3.57 us  [local(): lax.all_to_all(down_parts, 'tensor', split_axis=0, concat_axis=2, tiled=T...]
    dot_general x1, matrix products: 5.15 us -> 1.68 us  [local(): jnp.dot(flat_piece, weight_in, preferred_element_type=jnp.float32)]
  transfers between devices with their start and end apart: 3 -> 2, of which waited for: 2 -> 2; matrix products, arithmetic and copies ran while one was open for 9% -> 3% of each run, Pallas kernels for 0% -> 0%
where the time goes in v1:
time: 298 us
  blocking collectives  211 us (71%)
  waiting for transfers between devices  53.6 us (18%)
  local copies, waits for them, and re-layouts  14.2 us (5%)
  starting transfers between devices  8 us (3%)
  matrix products  6.54 us (2%)
  other arithmetic  4.47 us (2%)
    all_to_all x1, blocking collectives, local(): lax.all_to_all(jnp.stack([arrived] * lax.axis_size('tensor')), 'tensor',...  139 us
    all_to_all x2, blocking collectives, exchange_in_order(): lax.all_to_all(parts, axes[k], split_axis=k, concat_axis=k, tiled=True)  39.4 us
    all_to_all x1, blocking collectives, local(): lax.all_to_all(expert_out, EXPERT, split_axis=0, concat_axis=0, tiled=True)  32.4 us
    all_to_all x1, waiting for transfers between devices, from_everyone(): lax.all_to_all(jnp.broadcast_to(x[None], (size, *x.shape)), axis, 0, 0, t...  31 us
    all_to_all x1, waiting for transfers between devices, local(): lax.all_to_all(down_parts, 'tensor', split_axis=0, concat_axis=2, tiled=T...  22.6 us
    reshape x1, local copies, waits for them, and re-layouts, local(): jnp.concatenate(lax.all_to_all(jnp.stack([arrived] * lax.axis_size('tenso...  6.08 us
  transfers between devices with their start and end apart: 2, of which 2 were waited for; matrix products, arithmetic and copies ran while one was open for 3% of the time, Pallas kernels for 0%

profile of v1, /device:TPU:64, one launch (start us, length us, event | category | flops | bytes accessed | tf_op | source)
XLA Modules:
  0.0 297.8 jit_solution(5482845722754498569)
XLA Ops:
  0.0 0.0 copy-start
  0.0 0.9 select_reduce_fusion.2
  0.9 0.8 select_reduce_fusion.1
  1.7 0.1 copy.49
  1.8 0.1 eq.68
  2.0 1.5 reduce-window.6
  3.4 0.3 slice_reduce_fusion
  3.7 0.1 bitcast_bitcast_fusion
  3.8 0.1 reduce_sum.50
  4.0 0.1 copy.52
  4.0 1.1 convert_reduce_fusion
  5.1 0.0 copy-done
  5.1 0.4 convolution_convert_fusion.1
  5.5 0.2 reshape_reshape_reshape.3
  5.8 0.1 copy.53
  5.9 4.3 %all_to_all.40 = bf16[16,2,1,18,640]{4,0,3,2,1:T(8,128)(2,1)S(1)} all-to-all(bf16[16,2,1,18,640]{4,0,3,2,1:T(8,128)(2,1)S(1)} %copy.53), channel_id=1, replica_groups=mesh['expert_0'=4,'expert_1'=4,'expert_2'=2,'tensor'=8,'dp'=2] {'expert_2'}, dimensions={1} | all-to-all | bytes 1474560 | tf_op jit(solution)/shard_map/all_to_all | solution.py:27
  10.2 0.6 copy.54
  10.8 35.1 %all_to_all.41 = bf16[16,2,1,18,640]{4,1,3,2,0:T(2,128)(2,1)S(1)} all-to-all(bf16[16,2,1,18,640]{4,1,3,2,0:T(2,128)(2,1)S(1)} %copy.54), channel_id=1, replica_groups=mesh['expert_0'=4,'expert_1'=4,'expert_2'=2,'tensor'=8,'dp'=2] {'expert_..., dimensions={0} | all-to-all | bytes 1474560 | tf_op jit(solution)/shard_map/all_to_all | solution.py:27
  45.8 0.5 copy.55
  46.3 0.3 stack_reshape_reshape.2
  46.6 0.6 stack.3
  47.3 138.9 %all_to_all.42 = bf16[8,32,18,640]{3,1,2,0:T(8,128)(2,1)} all-to-all(bf16[8,32,18,640]{3,1,2,0:T(8,128)(2,1)S(1)} %stack.3), channel_id=1, replica_groups=mesh['expert_0'=4,'expert_1'=4,'expert_2'=2,'tensor'=8,'dp'=2] {'tensor'}, dimensions={0} | all-to-all | bytes 11796480 | tf_op jit(solution)/shard_map/all_to_all | solution.py:79
  186.2 3.6 %all-to-all-start.4 = ((bf16[8,640,128]{2,1,0:T(8,128)(2,1)}), bf16[8,640,128]{2,1,0:T(8,128)(2,1)S(1)}, u32[]{:S(2)}, u32[]{:S(2)}) async-start(bf16[8,640,128]{2,1,0:T(8,128)(2,1)} %bitcast.3), calls=%async_computation.4 | async-start | bytes 2621440 | tf_op jit(solution)/shard_map/all_to_all | solution.py:85
  189.8 6.1 %copy.56 = bf16[32,18,8,640]{3,2,1,0:T(8,128)(2,1)S(1)} copy(bf16[32,18,8,640]{3,0,1,2:T(8,128)(2,1)} %bitcast.43) | data formatting | bytes 11796480 | tf_op jit(solution)/shard_map/reshape | solution.py:78
  195.8 0.0 copy-start.1
  195.8 1.4 copy.62
  197.2 0.4 copy-done.1
  197.6 1.7 fusion
  199.3 0.1 fusion.5
  199.4 22.6 %all-to-all-done.4 = bf16[8,640,128]{2,1,0:T(8,128)(2,1)S(1)} async-done(((bf16[8,640,128]{2,1,0:T(8,128)(2,1)}), bf16[8,640,128]{2,1,0:T(8,128)(2,1)S(1)}, u32[]{:S(2)}, u32[]{:S(2)}) %all-to-all-start.4) | async-done | bytes 1310752 | tf_op jit(solution)/shard_map/all_to_all | solution.py:85
  221.9 1.2 broadcast_in_dim.58
  223.1 4.4 %all-to-all-start.3 = ((bf16[8,576,128]{2,1,0:T(8,128)(2,1)}), bf16[8,576,128]{2,1,0:T(8,128)(2,1)}, u32[]{:S(2)}, u32[]{:S(2)}) async-start(bf16[8,576,128]{2,1,0:T(8,128)(2,1)} %broadcast_in_dim.58), calls=%async_computation.3 | async-start | bytes 2359296 | tf_op jit(solution)/shard_map/all_to_all | solution.py:39
  227.6 0.7 copy.58
  228.3 31.0 %all-to-all-done.3 = bf16[8,576,128]{2,1,0:T(8,128)(2,1)} async-done(((bf16[8,576,128]{2,1,0:T(8,128)(2,1)}), bf16[8,576,128]{2,1,0:T(8,128)(2,1)}, u32[]{:S(2)}, u32[]{:S(2)}) %all-to-all-start.3) | async-done | bytes 1179680 | tf_op jit(solution)/shard_map/all_to_all | solution.py:39
  259.3 3.3 %convolution_convert_fusion = bf16[576,640]{1,0:T(8,128)(2,1)} fusion(bf16[640,1024]{0,1:T(8,128)(2,1)S(1)} %bitcast.47, bf16[8,576,128]{2,1,0:T(8,128)(2,1)} %all-to-all-done.3), kind=kOutput, calls=%fused_computation.6 | convolution fusion | flops 755343360 | bytes 3227648 | tf_op jit(solution)/shard_map/dot_general | solution.py:88
  262.6 1.3 reshape.63
  263.9 32.4 %all_to_all.43 = bf16[32,18,640]{2,1,0:T(8,128)(2,1)S(1)} all-to-all(bf16[32,18,640]{2,1,0:T(8,128)(2,1)S(1)} %reshape.63), channel_id=1, replica_groups=mesh['expert_0'=4,'expert_1'=4,'expert_2'=2,'tensor'=8,'dp'=2] {'expert_..., dimensions={0} | all-to-all | bytes 1474560 | tf_op jit(solution)/shard_map/all_to_all | solution.py:95
  296.3 0.2 reshape.64
  296.6 1.2 convolution_convert_fusion.2
  (5 shorter events, 0.1 us)
Async XLA Ops:
  0.0 5.1 %copy-start = (bf16[96,640]{1,0:T(8,128)(2,1)S(1)}, bf16[96,640]{1,0:T(8,128)(2,1)}, u32[]{:S(2)}) copy-start(bf16[96,640]{1,0:T(8,128)(2,1)} %param.7) | copy-start | bytes 368644
  186.2 35.8 %all-to-all-start.4 = ((bf16[8,640,128]{2,1,0:T(8,128)(2,1)}), bf16[8,640,128]{2,1,0:T(8,128)(2,1)S(1)}, u32[]{:S(2)}, u32[]{:S(2)}) async-start(bf16[8,640,128]{2,1,0:T(8,128)(2,1)} %bitcast.3), calls=%async_computation.4 | async-start | bytes 2621440 | tf_op jit(solution)/shard_map/all_to_all | solution.py:85
  195.8 1.7 copy-start.1
  223.1 36.2 %all-to-all-start.3 = ((bf16[8,576,128]{2,1,0:T(8,128)(2,1)}), bf16[8,576,128]{2,1,0:T(8,128)(2,1)}, u32[]{:S(2)}, u32[]{:S(2)}) async-start(bf16[8,576,128]{2,1,0:T(8,128)(2,1)} %broadcast_in_dim.58), calls=%async_computation.3 | async-start | bytes 2359296 | tf_op jit(solution)/shard_map/all_to_all | solution.py:39
